TPU v7x, 256 devices: a whole 4x4x8 slice. The times are simulated.
256 devices in a mesh: section: 16 (over y_hi, x, core), ray: 8 (over z), dp: 2 (over y_lo).
Axes of the slice: x: 4, y: 4 (y_hi: 2, y_lo: 2; y = y_hi * 2 + y_lo), z: 8, core: 2. Of those that a mesh axis runs over, the one named last changes fastest.
Arguments:
- section_tokens: bfloat16 [16, 2, 1024, 1024], P('section', 'dp', 'ray'), may hold values from -6 to 6
- enc_ln1: float32 [16, 1024], P('section'), may hold values from 0.5 to 1.5
- enc_qkv: bfloat16 [16, 1024, 3, 1024], P('section', None, None, 'ray'), may hold values from -40 to 40
- enc_out: bfloat16 [16, 1024, 1024], P('section', 'ray'), may hold values from -0.1875 to 0.1875
- enc_ln2: float32 [16, 1024], P('section'), may hold values from 0.5 to 1.5
- enc_up: bfloat16 [16, 1024, 4096], P('section', None, 'ray'), may hold values from -0.1875 to 0.1875
- enc_down: bfloat16 [16, 4096, 1024], P('section', 'ray'), may hold values from -0.09375 to 0.09375
- set_latent: bfloat16 [2, 1024, 1024], P('dp', 'ray'), may hold values from -6 to 6
- ray_queries: bfloat16 [2, 32768, 1024], P('dp', ('section', 'ray')), may hold values from -6 to 6
- dec_query: bfloat16 [1024, 1024], P('section'), may hold values from -40 to 40
- dec_kv: bfloat16 [1024, 2, 1024], P('section'), may hold values from -1 to 1
- dec_out: bfloat16 [1024, 1024], P('section'), may hold values from -0.1875 to 0.1875
- feature_grad: bfloat16 [2, 32768, 1024], P('dp', ('section', 'ray')), may hold values from -2 to 2
Outputs:
- handed: bfloat16 [16, 2, 1024, 1024], P('section', 'dp', 'ray')
- finished: bfloat16 [2, 1024, 1024], P('dp', 'ray', 'section')
- ray_features: bfloat16 [2, 32768, 1024], P('dp', ('section', 'ray'))
- latent_grad: bfloat16 [2, 1024, 1024], P('dp', 'ray')
- out_grad: float32 [1024, 1024], replicated
All inputs are finite; a program needn't handle non-finite values.
Results may differ from a plain program's by a relative error of at most 0.022.
The roundings to bfloat16 on the way count: a program that leaves them out, or rounds other values in their place, can miss the bound.
Values may be sent and summed in bfloat16 or wider, within the bound.
No kernel may reach another device: no remote copies, remote signals or barrier semaphores. Data moves between devices by JAX's collectives and lax.ppermute only.
A program may use at most 128 MiB of HBM per device.

v0:
```python
import math
import jax
import jax.numpy as jnp
from jax import lax
from jax.sharding import PartitionSpec as P

HEADS = 16


def shifted(value, axis, by):
    count = lax.axis_size(axis)
    pairs = [(i, i + by) for i in range(count) if 0 <= i + by < count]
    return lax.ppermute(value, axis, pairs)


def spread_2(value, axis, root):
    mine = lax.axis_index(axis) == root
    return lax.psum(jnp.where(mine, value, jnp.zeros_like(value)), axis)


def layer_norm(values, gain):
    values = values.astype(jnp.float32)
    center = values - jnp.mean(values, -1, keepdims=True)
    spread = jnp.mean(center * center, -1, keepdims=True)
    return center * lax.rsqrt(spread + 1e-05) * gain


def softmax_rows(scores):
    top = jnp.max(scores, -1, keepdims=True)
    expo = jnp.exp(scores - top)
    return expo / jnp.sum(expo, -1, keepdims=True)


def attend_heads(packed, head_dim):
    length = packed.shape[0]
    heads = packed.shape[1] // (3 * head_dim)
    split = packed.reshape(length, 3, heads, head_dim)
    scores = jnp.einsum(
        "qhd,khd->hqk", split[:, 0], split[:, 1], preferred_element_type=jnp.float32
    ) / math.sqrt(head_dim)
    probs = softmax_rows(scores).astype(jnp.bfloat16)
    mixed = jnp.einsum("hqk,khd->qhd", probs, split[:, 2], preferred_element_type=jnp.float32)
    return mixed.astype(jnp.bfloat16).reshape(length, heads * head_dim)


def latent_rows(pair_sum, w_pairs):
    result = lax.dot_general(
        pair_sum[:, 0],
        w_pairs[:, 0, :],
        (((1,), (1,)), ((), ())),
        preferred_element_type=jnp.float32,
    )
    result = result + lax.dot_general(
        pair_sum[:, 1],
        w_pairs[:, 1, :],
        (((1,), (1,)), ((), ())),
        preferred_element_type=jnp.float32,
    )
    return result.astype(jnp.bfloat16)


def local(
    section_tokens,
    enc_ln1,
    enc_qkv,
    enc_out,
    enc_ln2,
    enc_up,
    enc_down,
    set_latent,
    ray_queries,
    dec_query,
    dec_kv,
    dec_out,
    feature_grad,
):
    tokens = section_tokens[0, 0]
    width = tokens.shape[1]
    head_dim = width // HEADS
    local_width = enc_out.shape[1]
    w_qkv = enc_qkv[0].reshape(width, 3 * local_width)
    w_attn_out = enc_out[0]
    w_upper = enc_up[0]
    w_lower = enc_down[0]
    gain_one = enc_ln1[0]
    gain_two = enc_ln2[0]
    normed = layer_norm(tokens, gain_one).astype(jnp.bfloat16)
    packed = jnp.dot(
        lax.all_gather(normed, "ray", axis=0, tiled=True), w_qkv, preferred_element_type=jnp.float32
    ).astype(jnp.bfloat16)
    mixed = attend_heads(packed, head_dim)
    attn_rows = lax.psum_scatter(
        jnp.dot(mixed, w_attn_out, preferred_element_type=jnp.float32).astype(jnp.bfloat16),
        "ray",
        scatter_dimension=0,
        tiled=True,
    ).astype(jnp.float32)
    hidden = (tokens.astype(jnp.float32) + attn_rows).astype(jnp.bfloat16)
    upper = jax.nn.gelu(
        jnp.dot(
            lax.all_gather(
                layer_norm(hidden, gain_two).astype(jnp.bfloat16), "ray", axis=0, tiled=True
            ),
            w_upper,
            preferred_element_type=jnp.float32,
        ),
        approximate=True,
    ).astype(jnp.bfloat16)
    lower_rows = lax.psum_scatter(
        jnp.dot(upper, w_lower, preferred_element_type=jnp.float32).astype(jnp.bfloat16),
        "ray",
        scatter_dimension=0,
        tiled=True,
    ).astype(jnp.float32)
    layer_out = (hidden.astype(jnp.float32) + lower_rows).astype(jnp.bfloat16)
    handed = shifted(layer_out, "section", 1)
    finished_all = spread_2(layer_out, "section", lax.axis_size("section") - 1)
    columns = width // lax.axis_size("section")
    finished = lax.dynamic_slice_in_dim(
        finished_all, lax.axis_index("section") * columns, columns, 1
    )
    w_query, w_pairs, w_mix = (
        lax.all_gather(dec_query, "section", axis=0, tiled=True),
        lax.all_gather(dec_kv, "section", axis=0, tiled=True),
        lax.all_gather(dec_out, "section", axis=0, tiled=True),
    )
    latent = set_latent[0]
    queries = ray_queries[0]
    cotangent = feature_grad[0]
    flat_pairs = w_pairs.reshape(width, 2 * width)
    key_values = lax.all_gather(
        jnp.dot(latent, flat_pairs, preferred_element_type=jnp.float32).astype(jnp.bfloat16),
        "ray",
        axis=0,
        tiled=True,
    )
    scene_len = key_values.shape[0]
    ray_rows = queries.shape[0]
    scale = 1.0 / math.sqrt(head_dim)
    keys = key_values[:, :width].reshape(scene_len, HEADS, head_dim)
    values = key_values[:, width:].reshape(scene_len, HEADS, head_dim)
    query = (
        jnp.dot(queries, w_query, preferred_element_type=jnp.float32)
        .astype(jnp.bfloat16)
        .reshape(ray_rows, HEADS, head_dim)
    )
    scores = jnp.einsum("rhd,lhd->hrl", query, keys, preferred_element_type=jnp.float32) * scale
    probs = softmax_rows(scores)
    probs_low = probs.astype(jnp.bfloat16)
    attended = (
        jnp.einsum("hrl,lhd->rhd", probs_low, values, preferred_element_type=jnp.float32)
        .astype(jnp.bfloat16)
        .reshape(ray_rows, width)
    )
    features = (
        queries.astype(jnp.float32) + jnp.dot(attended, w_mix, preferred_element_type=jnp.float32)
    ).astype(jnp.bfloat16)
    mix_term = lax.dot_general(
        attended, cotangent, (((0,), (0,)), ((), ())), preferred_element_type=jnp.float32
    )
    out_grad = lax.psum(mix_term, ("section", "ray", "dp"))
    attn_grad = lax.dot_general(
        cotangent, w_mix, (((1,), (1,)), ((), ())), preferred_element_type=jnp.float32
    )
    attn_grad = attn_grad.astype(jnp.bfloat16).reshape(ray_rows, HEADS, head_dim)
    prob_grad = jnp.einsum("rhd,lhd->hrl", attn_grad, values, preferred_element_type=jnp.float32)
    delta = jnp.sum(probs * prob_grad, -1, keepdims=True)
    score_grad = (probs * (prob_grad - delta) * scale).astype(jnp.bfloat16)
    count = latent.shape[0] * lax.axis_size("ray")
    key_grad = jnp.einsum(
        "hrl,rhd->lhd", score_grad, query, preferred_element_type=jnp.float32
    ).reshape(count, width)
    value_grad = jnp.einsum(
        "hrl,rhd->lhd", probs_low, attn_grad, preferred_element_type=jnp.float32
    ).reshape(count, width)
    stacked = jnp.stack([key_grad, value_grad], 1)
    pair_rows = lax.psum_scatter(
        stacked.astype(jnp.bfloat16), "ray", scatter_dimension=0, tiled=True
    )
    pair_sum = lax.psum(pair_rows, "section")
    latent_grad = latent_rows(pair_sum, w_pairs)
    return (handed[None, None], finished[None], features[None], latent_grad[None], out_grad)


def solution(mesh):
    return jax.shard_map(
        local,
        mesh=mesh,
        in_specs=(
            P("section", "dp", "ray", None),
            P("section", None),
            P("section", None, None, "ray"),
            P("section", "ray", None),
            P("section", None),
            P("section", None, "ray"),
            P("section", "ray", None),
            P("dp", "ray", None),
            P("dp", ("section", "ray"), None),
            P("section", None),
            P("section", None, None),
            P("section", None),
            P("dp", ("section", "ray"), None),
        ),
        out_specs=(
            P("section", "dp", "ray", None),
            P("dp", "ray", "section"),
            P("dp", ("section", "ray"), None),
            P("dp", "ray", None),
            P(),
        ),
        check_vma=False,
    )
```

profile of v0, /device:TPU:2, one launch (start us, length us, event | category | flops | bytes accessed | tf_op | source)
XLA Modules:
  0.0 928.3 jit_solution(4946242236666145838)
XLA Ops:
  13.8 42.5 %all-gather.7.cloned.1.call-done = bf16[1024,1024]{1,0:T(8,128)(2,1)} async-done(((bf16[128,1024]{1,0:T(8,128)(2,1)}), bf16[1024,1024]{1,0:T(8,128)(2,1)}) %all-gather.7.cloned.1.call-update) | async-done | bytes 2097168 | tf_op jit(solution)/shard_map/all_gather | solution.py:89
  58.9 4.9 fusion.97
  63.7 4.3 fusion.48
  71.9 39.7 %reduce-scatter.6.cloned.1.call-done = bf16[128,1024]{1,0:T(8,128)(2,1)} async-done(((bf16[1024,1024]{1,0:T(8,128)(2,1)}), bf16[128,1024]{1,0:T(8,128)(2,1)}) %reduce-scatter.6.cloned.1.call-update) | async-done | bytes 262160 | tf_op jit(solution)/shard_map/reduce_scatter | solution.py:92
  114.0 18.6 %all-gather.11.cloned.1.call-done = bf16[1024,2,1024]{2,1,0:T(2,128)(2,1)} async-done(((bf16[64,2,1024]{2,1,0:T(2,128)(2,1)}), bf16[1024,2,1024]{2,1,0:T(2,128)(2,1)}) %all-gather.11.cloned.1.call-update) | async-done | bytes 4194320 | tf_op jit(solution)/shard_map/all_gather | solution.py:124
  132.7 11.1 %copy.47 = bf16[1024,2,1024]{0,2,1:T(8,128)(2,1)} copy(bf16[1024,2,1024]{2,1,0:T(2,128)(2,1)} %all-gather.11.cloned.1.call-done) | data formatting | bytes 8388608 | tf_op jit(solution)/shard_map/all_gather | solution.py:124
  143.8 4.6 convolution_convert_fusion
  148.5 39.0 %all-gather.15.cloned.1.call-done = bf16[1024,1024]{1,0:T(8,128)(2,1)} async-done(((bf16[64,1024]{1,0:T(8,128)(2,1)}), bf16[1024,1024]{1,0:T(8,128)(2,1)}) %all-gather.15.cloned.1.call-update) | async-done | bytes 2097168 | tf_op jit(solution)/shard_map/all_gather | solution.py:123
  190.8 51.5 %all-gather.17.cloned.1.call-done = bf16[1024,1024]{1,0:T(8,128)(2,1)} async-done(((bf16[64,1024]{1,0:T(8,128)(2,1)}), bf16[1024,1024]{1,0:T(8,128)(2,1)}) %all-gather.17.cloned.1.call-update) | async-done | bytes 2097168 | tf_op jit(solution)/shard_map/all_gather | solution.py:125
  245.6 39.2 %all-gather.9.cloned.1.call-done = bf16[1024,1024]{1,0:T(8,128)(2,1)} async-done(((bf16[128,1024]{1,0:T(8,128)(2,1)}), bf16[1024,1024]{1,0:T(8,128)(2,1)}) %all-gather.9.cloned.1.call-update) | async-done | bytes 2097168 | tf_op jit(solution)/shard_map/all_gather | solution.py:101
  284.9 5.8 convolution_convert_fusion.1
  290.9 66.2 %all-gather.13.cloned.1.call-done = bf16[1024,2048]{1,0:T(8,128)(2,1)} async-done(((bf16[128,2048]{1,0:T(8,128)(2,1)}), bf16[1024,2048]{1,0:T(8,128)(2,1)}) %all-gather.13.cloned.1.call-update) | async-done | bytes 4194320 | tf_op jit(solution)/shard_map/all_gather | solution.py:131
  366.7 9.8 %fusion.98 = (f32[16,256]{1,0:T(8,128)S(1)}, f32[16,256,1024]{2,1,0:T(8,128)}) fusion(bf16[256,16,64]{0,2,1:T(8,128)(2,1)S(1)} %bitcast.149, bf16[1024,16,64]{0,2,1:T(8,128)(2,1)} %bitcast.144), kind=kOutput, calls=%fused_computation.110 | convolution fusion | flops 549454848 | bytes 19415040 | tf_op jit(solution)/shard_map/sub | solution.py:30
  376.5 8.1 fusion.99
  384.5 38.2 %fusion.38 = bf16[16,64,1024]{2,1,0:T(8,128)(2,1)} fusion(bf16[256,16,64]{0,2,1:T(8,128)(2,1)S(1)} %bitcast.150, f32[16,256,1024]{2,1,0:T(8,128)} %fusion.99, f32[16,256,1024]{2,1,0:T(8,128)} %get-tuple-element.18, f32[16,256]{1,0:T(8,128)S(1)} %get-tuple-element.17), kind=kOutput, calls=%fused_computation.40 | convolution fusion | flops 567284736 | bytes 36192256 | tf_op jit(solution)/shard_map/hrl,rhd->lhd/dot_general | solution.py:170
  422.8 7.1 fusion.35
  432.3 6.5 copy.57
  440.8 52.2 %reduce-scatter.10.cloned.1.call-done = bf16[128,2048]{1,0:T(8,128)(2,1)} async-done(((bf16[1024,2048]{1,0:T(8,128)(2,1)}), bf16[128,2048]{1,0:T(8,128)(2,1)}) %reduce-scatter.10.cloned.1.call-update) | async-done | bytes 524304
  495.3 8.5 fusion.42
  506.5 10.0 %fusion.95 = (bf16[1024,1,1024]{2,1,0:T(2,128)(2,1)}, bf16[1024,1,1024]{2,1,0:T(2,128)(2,1)}) fusion(bf16[1024,2,1024]{2,1,0:T(2,128)(2,1)} %all-gather.11.cloned.1.call-done), kind=kLoop, calls=%fused_computation.107 | loop fusion | bytes 8388608 | tf_op jit(solution)/shard_map/slice | solution.py:49
  520.0 4.7 collective-permute-done
  524.7 109.9 %all-reduce.6.cloned.1.call-done = (bf16[128,1024]{1,0:T(8,128)(2,1)}, bf16[128,2,1024]{0,2,1:T(8,128)(2,1)}) async-done(((bf16[128,1024]{1,0:T(8,128)(2,1)}, bf16[128,2,1024]{0,2,1:T(8,128)(2,1)}), (bf16[128,1024]{1,0:T(8,128)(2,1)}, bf16[128,2,1024]{0,2,1:T(8,128)(2,1)})) %all-reduce.6.cloned.1.call-update) | async-done | bytes 786448 | tf_op jit(solution)/shard_map/psum | solution.py:18
  643.2 272.5 %all-reduce.4.cloned.1.call-done = f32[1024,1024]{1,0:T(8,128)} async-done(((f32[1024,1024]{1,0:T(8,128)}), f32[1024,1024]{1,0:T(8,128)}) %all-reduce.4.cloned.1.call-update) | async-done | bytes 4194320 | tf_op jit(solution)/shard_map/psum | solution.py:161
  916.4 4.8 copy.76
  (84 shorter events, 52.9 us)
Async XLA Ops:
  8.0 276.9 %copy-start = (bf16[1,512,1024]{2,1,0:T(8,128)(2,1)S(1)}, bf16[1,512,1024]{2,1,0:T(8,128)(2,1)}, u32[]{:S(2)}) copy-start(bf16[1,512,1024]{2,1,0:T(8,128)(2,1)} %param.19) | copy-start | bytes 3145732
  8.0 48.2 %all-gather.7.cloned.1.call-start = ((), (), s32[]{:S(2)}) async-start(), calls=%async_computation.3 | async-start | bytes 2359296 | tf_op jit(solution)/shard_map/all_gather | solution.py:89
  12.3 99.4 %reduce-scatter.6.cloned.1.call-start = ((), (), s32[]{:S(2)}) async-start(), calls=%async_computation.4 | async-start | bytes 2359296 | tf_op jit(solution)/shard_map/reduce_scatter | solution.py:92
  68.0 43.6 %copy-start.2 = (bf16[1,1,128,1024]{3,2,1,0:T(8,128)(2,1)S(1)}, bf16[1,1,128,1024]{3,2,1,0:T(8,128)(2,1)}, u32[]{:S(2)}) copy-start(bf16[1,1,128,1024]{3,2,1,0:T(8,128)(2,1)} %param.13) | copy-start | bytes 786436
  68.0 45.0 %copy-start.14 = (f32[1,1024]{1,0:T(1,128)S(1)}, f32[1,1024]{1,0:T(1,128)}, u32[]{:S(2)}) copy-start(f32[1,1024]{1,0:T(1,128)} %param.17) | copy-start | bytes 12292
  70.1 62.5 %all-gather.11.cloned.1.call-start = ((), (), s32[]{:S(2)}) async-start(), calls=%async_computation.7 | async-start | bytes 4456448 | tf_op jit(solution)/shard_map/all_gather | solution.py:124
  70.7 116.8 %all-gather.15.cloned.1.call-start = ((), (), s32[]{:S(2)}) async-start(), calls=%async_computation.9 | async-start | bytes 2228224 | tf_op jit(solution)/shard_map/all_gather | solution.py:123
  71.3 171.0 %all-gather.17.cloned.1.call-start = ((), (), s32[]{:S(2)}) async-start(), calls=%async_computation.10 | async-start | bytes 2228224 | tf_op jit(solution)/shard_map/all_gather | solution.py:125
  71.9 213.0 %all-gather.9.cloned.1.call-start = ((), (), s32[]{:S(2)}) async-start(), calls=%async_computation.5 | async-start | bytes 2359296 | tf_op jit(solution)/shard_map/all_gather | solution.py:101
  114.0 29.8 %copy-start.12 = (bf16[1,128,1024]{2,1,0:T(8,128)(2,1)S(1)}, bf16[1,128,1024]{2,1,0:T(8,128)(2,1)}, u32[]{:S(2)}) copy-start(bf16[1,128,1024]{2,1,0:T(8,128)(2,1)} %param.20) | copy-start | bytes 786436
  114.0 243.2 %all-gather.13.cloned.1.call-start = ((), (), s32[]{:S(2)}) async-start(), calls=%async_computation.8 | async-start | bytes 4718592 | tf_op jit(solution)/shard_map/all_gather | solution.py:131
  143.8 43.7 %copy-start.8 = (bf16[1,256,1024]{2,1,0:T(8,128)(2,1)S(1)}, bf16[1,256,1024]{2,1,0:T(8,128)(2,1)}, u32[]{:S(2)}) copy-start(bf16[1,256,1024]{2,1,0:T(8,128)(2,1)} %param.21) | copy-start | bytes 1572868
  143.8 98.5 %copy-start.6 = (bf16[1,256,1024]{2,1,0:T(8,128)(2,1)S(1)}, bf16[1,256,1024]{2,1,0:T(8,128)(2,1)}, u32[]{:S(2)}) copy-start(bf16[1,256,1024]{2,1,0:T(8,128)(2,1)} %param.25) | copy-start | bytes 1572868
  148.5 290.5 %reduce-scatter.8.cloned.1.call-start = ((), (), s32[]{:S(2)}) async-start(), calls=%async_computation.6 | async-start | bytes 2359296 | tf_op jit(solution)/shard_map/reduce_scatter | solution.py:109
  290.7 202.2 %reduce-scatter.10.cloned.1.call-start = ((), (), s32[]{:S(2)}) async-start(), calls=%async_computation.12 | async-start | bytes 4718592
  366.6 9.8 %copy-start.4 = (bf16[256,1024]{0,1:T(8,128)(2,1)S(1)}, bf16[256,1024]{0,1:T(8,128)(2,1)}, u32[]{:S(2)}) copy-start(bf16[256,1024]{0,1:T(8,128)(2,1)} %copy.51) | copy-start | bytes 1572868
  422.8 7.1 copy-start.5
  438.8 195.8 %all-reduce.6.cloned.1.call-start = ((), (), s32[]{:S(2)}) async-start(), calls=%async_computation.13 | async-start | bytes 1572864 | tf_op jit(solution)/shard_map/psum | solution.py:18
  495.0 8.8 copy-start.7
  495.0 420.7 %all-reduce.4.cloned.1.call-start = ((), (), s32[]{:S(2)}) async-start(), calls=%async_computation.11 | async-start | bytes 8388608 | tf_op jit(solution)/shard_map/psum | solution.py:161
  506.5 10.0 %copy-start.13 = (bf16[128,1024]{1,0:T(8,128)(2,1)S(1)}, bf16[128,1024]{1,0:T(8,128)(2,1)}, u32[]{:S(2)}) copy-start(bf16[128,1024]{1,0:T(8,128)(2,1)} %get-tuple-element.8) | copy-start | bytes 786436
  506.5 11.9 %copy-start.3 = (bf16[1024,1024]{1,0:T(8,128)(2,1)S(1)}, bf16[1024,1024]{1,0:T(8,128)(2,1)}, u32[]{:S(2)}) copy-start(bf16[1024,1024]{1,0:T(8,128)(2,1)} %all-gather.17.cloned.1.call-done) | copy-start | bytes 6291460
  506.5 11.9 %copy-start.9 = (bf16[1,256,1024]{2,1,0:T(8,128)(2,1)S(1)}, bf16[1,256,1024]{2,1,0:T(8,128)(2,1)}, u32[]{:S(2)}) copy-start(bf16[1,256,1024]{2,1,0:T(8,128)(2,1)} %param.21) | copy-start | bytes 1572868
  516.5 8.2 collective-permute-start
  (3 other events, 15.2 us)
Sparse Core Ops, SparseCore 0:
  12.4 43.7 all-gather.6
  70.3 41.3 reduce-scatter.5
  290.8 69.1 reduce-scatter.7
  439.0 53.9 reduce-scatter.9
Sparse Core Ops, SparseCore 1:
  73.4 59.3 all-gather.10
  135.3 52.1 all-gather.14
  190.1 52.1 all-gather.16
  244.7 40.1 all-gather.8
  286.7 70.4 all-gather.12
  495.1 139.5 all-reduce.5
  640.0 275.7 all-reduce.3
where the time goes:
time: 929 us; the launch traced here: 928 us
  waiting for transfers between devices  738 us (79%)
  matrix products  112 us (12%)
  local copies, waits for them, and re-layouts  49.6 us (5%)
  between operations  15.6 us (2%)
  other arithmetic  10.7 us (1%)
    psum x1, waiting for transfers between devices, local(): out_grad = lax.psum(mix_term, ('section', 'ray', 'dp'))  273 us
    psum x1, waiting for transfers between devices, spread_2(): return lax.psum(jnp.where(mine, value, jnp.zeros_like(value)), axis)  110 us
    all_gather x1, waiting for transfers between devices, local(): lax.all_gather(jnp.dot(latent, flat_pairs, preferred_element_type=jnp.flo...  66.2 us
    unnamed x12, waiting for transfers between devices  53.9 us
    all_gather x1, waiting for transfers between devices, local(): lax.all_gather(dec_out, 'section', axis=0, tiled=True)  51.5 us
    all_gather x1, waiting for transfers between devices, local(): lax.all_gather(normed, 'ray', axis=0, tiled=True)  42.5 us
    reduce_scatter x1, waiting for transfers between devices, local(): lax.psum_scatter(jnp.dot(mixed, w_attn_out, preferred_element_type=jnp.fl...  39.7 us
    all_gather x1, waiting for transfers between devices, local(): lax.all_gather(layer_norm(hidden, gain_two).astype(jnp.bfloat16), 'ray',...  39.2 us
  transfers between devices with their start and end apart: 12, of which 11 were waited for; matrix products, arithmetic and copies ran while one was open for 16% of the time, Pallas kernels for 0%

commit v1 on v0

--- a/solution.py
+++ b/solution.py
@@ -158,7 +158,8 @@
     mix_term = lax.dot_general(
         attended, cotangent, (((0,), (0,)), ((), ())), preferred_element_type=jnp.float32
     )
-    out_grad = lax.psum(mix_term, ("section", "ray", "dp"))
+    partial = lax.psum(mix_term, "section")
+    out_grad = lax.psum(partial, ("ray", "dp"))
     attn_grad = lax.dot_general(
         cotangent, w_mix, (((1,), (1,)), ((), ())), preferred_element_type=jnp.float32
     )

time: 929 us -> 972 us (1.046)
  waiting for transfers between devices: 738 us -> 780 us
    psum x1 -> x2, waiting for transfers between devices: 273 us -> 305 us  [the longest x1 200 us: local(): out_grad = lax.psum(partial, ('ray', 'dp'))]
    psum x1, waiting for transfers between devices: 110 us -> 129 us  [spread_2(): return lax.psum(jnp.where(mine, value, jnp.zeros_like(value)), axis)]
    unnamed x12 -> x13, waiting for transfers between devices: 53.9 us -> 42.4 us
  transfers between devices with their start and end apart: 12 -> 13, of which waited for: 11 -> 12; matrix products, arithmetic and copies ran while one was open for 16% -> 15% of each run, Pallas kernels for 0% -> 0%
where the time goes in v1:
time: 972 us; the launch traced here: 971 us
  waiting for transfers between devices  780 us (80%)
  matrix products  112 us (12%)
  local copies, waits for them, and re-layouts  49.6 us (5%)
  between operations  15.6 us (2%)
  other arithmetic  10.6 us (1%)
    psum x1, waiting for transfers between devices, local(): out_grad = lax.psum(partial, ('ray', 'dp'))  200 us
    psum x1, waiting for transfers between devices, spread_2(): return lax.psum(jnp.where(mine, value, jnp.zeros_like(value)), axis)  129 us
    psum x1, waiting for transfers between devices, local(): partial = lax.psum(mix_term, 'section')  104 us
    all_gather x1, waiting for transfers between devices, local(): lax.all_gather(jnp.dot(latent, flat_pairs, preferred_element_type=jnp.flo...  66.3 us
    all_gather x1, waiting for transfers between devices, local(): lax.all_gather(dec_out, 'section', axis=0, tiled=True)  51.5 us
    all_gather x1, waiting for transfers between devices, local(): lax.all_gather(normed, 'ray', axis=0, tiled=True)  42.5 us
    unnamed x13, waiting for transfers between devices  42.4 us
    reduce_scatter x1, waiting for transfers between devices, local(): lax.psum_scatter(jnp.dot(mixed, w_attn_out, preferred_element_type=jnp.fl...  39.8 us
  transfers between devices with their start and end apart: 13, of which 12 were waited for; matrix products, arithmetic and copies ran while one was open for 15% of the time, Pallas kernels for 0%

profile of v1, /device:TPU:2, one launch (start us, length us, event | category | flops | bytes accessed | tf_op | source)
XLA Modules:
  0.0 970.8 jit_solution(2971991846381023970)
XLA Ops:
  13.8 42.5 %all-gather.7.cloned.1.call-done = bf16[1024,1024]{1,0:T(8,128)(2,1)} async-done(((bf16[128,1024]{1,0:T(8,128)(2,1)}), bf16[1024,1024]{1,0:T(8,128)(2,1)}) %all-gather.7.cloned.1.call-update) | async-done | bytes 2097168 | tf_op jit(solution)/shard_map/all_gather | solution.py:89
  58.9 4.9 fusion.97
  71.9 39.8 %reduce-scatter.6.cloned.1.call-done = bf16[128,1024]{1,0:T(8,128)(2,1)} async-done(((bf16[1024,1024]{1,0:T(8,128)(2,1)}), bf16[128,1024]{1,0:T(8,128)(2,1)}) %reduce-scatter.6.cloned.1.call-update) | async-done | bytes 262160 | tf_op jit(solution)/shard_map/reduce_scatter | solution.py:92
  114.1 18.6 %all-gather.11.cloned.1.call-done = bf16[1024,2,1024]{2,1,0:T(2,128)(2,1)} async-done(((bf16[64,2,1024]{2,1,0:T(2,128)(2,1)}), bf16[1024,2,1024]{2,1,0:T(2,128)(2,1)}) %all-gather.11.cloned.1.call-update) | async-done | bytes 4194320 | tf_op jit(solution)/shard_map/all_gather | solution.py:124
  132.7 11.1 %copy.47 = bf16[1024,2,1024]{0,2,1:T(8,128)(2,1)} copy(bf16[1024,2,1024]{2,1,0:T(2,128)(2,1)} %all-gather.11.cloned.1.call-done) | data formatting | bytes 8388608 | tf_op jit(solution)/shard_map/all_gather | solution.py:124
  143.8 4.6 convolution_convert_fusion
  148.5 39.0 %all-gather.15.cloned.1.call-done = bf16[1024,1024]{1,0:T(8,128)(2,1)} async-done(((bf16[64,1024]{1,0:T(8,128)(2,1)}), bf16[1024,1024]{1,0:T(8,128)(2,1)}) %all-gather.15.cloned.1.call-update) | async-done | bytes 2097168 | tf_op jit(solution)/shard_map/all_gather | solution.py:123
  190.8 51.5 %all-gather.17.cloned.1.call-done = bf16[1024,1024]{1,0:T(8,128)(2,1)} async-done(((bf16[64,1024]{1,0:T(8,128)(2,1)}), bf16[1024,1024]{1,0:T(8,128)(2,1)}) %all-gather.17.cloned.1.call-update) | async-done | bytes 2097168 | tf_op jit(solution)/shard_map/all_gather | solution.py:125
  245.6 39.2 %all-gather.9.cloned.1.call-done = bf16[1024,1024]{1,0:T(8,128)(2,1)} async-done(((bf16[128,1024]{1,0:T(8,128)(2,1)}), bf16[1024,1024]{1,0:T(8,128)(2,1)}) %all-gather.9.cloned.1.call-update) | async-done | bytes 2097168 | tf_op jit(solution)/shard_map/all_gather | solution.py:101
  284.9 5.8 convolution_convert_fusion.1
  290.9 66.3 %all-gather.13.cloned.1.call-done = bf16[1024,2048]{1,0:T(8,128)(2,1)} async-done(((bf16[128,2048]{1,0:T(8,128)(2,1)}), bf16[1024,2048]{1,0:T(8,128)(2,1)}) %all-gather.13.cloned.1.call-update) | async-done | bytes 4194320 | tf_op jit(solution)/shard_map/all_gather | solution.py:131
  366.6 9.8 %fusion.98 = (f32[16,256]{1,0:T(8,128)S(1)}, f32[16,256,1024]{2,1,0:T(8,128)}) fusion(bf16[256,16,64]{0,2,1:T(8,128)(2,1)S(1)} %bitcast.149, bf16[1024,16,64]{0,2,1:T(8,128)(2,1)} %bitcast.144), kind=kOutput, calls=%fused_computation.110 | convolution fusion | flops 549454848 | bytes 19415040 | tf_op jit(solution)/shard_map/sub | solution.py:30
  376.5 8.1 fusion.99
  384.6 38.2 %fusion.38 = bf16[16,64,1024]{2,1,0:T(8,128)(2,1)} fusion(bf16[256,16,64]{0,2,1:T(8,128)(2,1)S(1)} %bitcast.150, f32[16,256,1024]{2,1,0:T(8,128)} %fusion.99, f32[16,256,1024]{2,1,0:T(8,128)} %get-tuple-element.18, f32[16,256]{1,0:T(8,128)S(1)} %get-tuple-element.17), kind=kOutput, calls=%fused_computation.40 | convolution fusion | flops 567284736 | bytes 36192256 | tf_op jit(solution)/shard_map/hrl,rhd->lhd/dot_general | solution.py:171
  422.7 7.1 fusion.35
  432.2 6.5 copy.57
  439.1 8.5 fusion.42
  452.2 40.7 %reduce-scatter.10.cloned.1.call-done = bf16[128,2048]{1,0:T(8,128)(2,1)} async-done(((bf16[1024,2048]{1,0:T(8,128)(2,1)}), bf16[128,2048]{1,0:T(8,128)(2,1)}) %reduce-scatter.10.cloned.1.call-update) | async-done | bytes 524304
  495.0 104.4 %all-reduce.5.cloned.1.call-done = f32[1024,1024]{1,0:T(8,128)} async-done(((f32[1024,1024]{1,0:T(8,128)}), f32[1024,1024]{1,0:T(8,128)}) %all-reduce.5.cloned.1.call-update) | async-done | bytes 4194320 | tf_op jit(solution)/shard_map/psum | solution.py:161
  599.4 10.0 %fusion.95 = (bf16[1024,1,1024]{2,1,0:T(2,128)(2,1)}, bf16[1024,1,1024]{2,1,0:T(2,128)(2,1)}) fusion(bf16[1024,2,1024]{2,1,0:T(2,128)(2,1)} %all-gather.11.cloned.1.call-done), kind=kLoop, calls=%fused_computation.107 | loop fusion | bytes 8388608 | tf_op jit(solution)/shard_map/slice | solution.py:49
  612.9 7.1 collective-permute-done
  620.0 129.4 %all-reduce.9.cloned.1.call-done = (bf16[128,1024]{1,0:T(8,128)(2,1)}, bf16[128,2,1024]{0,2,1:T(8,128)(2,1)}) async-done(((bf16[128,1024]{1,0:T(8,128)(2,1)}, bf16[128,2,1024]{0,2,1:T(8,128)(2,1)}), (bf16[128,1024]{1,0:T(8,128)(2,1)}, bf16[128,2,1024]{0,2,1:T(8,128)(2,1)})) %all-reduce.9.cloned.1.call-update) | async-done | bytes 786448 | tf_op jit(solution)/shard_map/psum | solution.py:18
  757.9 200.3 %all-reduce.7.cloned.1.call-done = f32[1024,1024]{1,0:T(8,128)} async-done(((f32[1024,1024]{1,0:T(8,128)}), f32[1024,1024]{1,0:T(8,128)}) %all-reduce.7.cloned.1.call-update) | async-done | bytes 4194320 | tf_op jit(solution)/shard_map/psum | solution.py:162
  958.9 4.8 copy.77
  (85 shorter events, 57.2 us)
Async XLA Ops:
  8.0 276.9 %copy-start = (bf16[1,512,1024]{2,1,0:T(8,128)(2,1)S(1)}, bf16[1,512,1024]{2,1,0:T(8,128)(2,1)}, u32[]{:S(2)}) copy-start(bf16[1,512,1024]{2,1,0:T(8,128)(2,1)} %param.19) | copy-start | bytes 3145732
  8.0 48.2 %all-gather.7.cloned.1.call-start = ((), (), s32[]{:S(2)}) async-start(), calls=%async_computation.3 | async-start | bytes 2359296 | tf_op jit(solution)/shard_map/all_gather | solution.py:89
  12.3 99.4 %reduce-scatter.6.cloned.1.call-start = ((), (), s32[]{:S(2)}) async-start(), calls=%async_computation.4 | async-start | bytes 2359296 | tf_op jit(solution)/shard_map/reduce_scatter | solution.py:92
  68.0 43.7 %copy-start.2 = (bf16[1,1,128,1024]{3,2,1,0:T(8,128)(2,1)S(1)}, bf16[1,1,128,1024]{3,2,1,0:T(8,128)(2,1)}, u32[]{:S(2)}) copy-start(bf16[1,1,128,1024]{3,2,1,0:T(8,128)(2,1)} %param.13) | copy-start | bytes 786436
  68.0 45.0 %copy-start.13 = (f32[1,1024]{1,0:T(1,128)S(1)}, f32[1,1024]{1,0:T(1,128)}, u32[]{:S(2)}) copy-start(f32[1,1024]{1,0:T(1,128)} %param.17) | copy-start | bytes 12292
  70.1 62.5 %all-gather.11.cloned.1.call-start = ((), (), s32[]{:S(2)}) async-start(), calls=%async_computation.7 | async-start | bytes 4456448 | tf_op jit(solution)/shard_map/all_gather | solution.py:124
  70.7 116.8 %all-gather.15.cloned.1.call-start = ((), (), s32[]{:S(2)}) async-start(), calls=%async_computation.9 | async-start | bytes 2228224 | tf_op jit(solution)/shard_map/all_gather | solution.py:123
  71.3 171.0 %all-gather.17.cloned.1.call-start = ((), (), s32[]{:S(2)}) async-start(), calls=%async_computation.10 | async-start | bytes 2228224 | tf_op jit(solution)/shard_map/all_gather | solution.py:125
  71.9 213.0 %all-gather.9.cloned.1.call-start = ((), (), s32[]{:S(2)}) async-start(), calls=%async_computation.5 | async-start | bytes 2359296 | tf_op jit(solution)/shard_map/all_gather | solution.py:101
  114.0 29.8 %copy-start.12 = (bf16[1,128,1024]{2,1,0:T(8,128)(2,1)S(1)}, bf16[1,128,1024]{2,1,0:T(8,128)(2,1)}, u32[]{:S(2)}) copy-start(bf16[1,128,1024]{2,1,0:T(8,128)(2,1)} %param.20) | copy-start | bytes 786436
  114.0 243.2 %all-gather.13.cloned.1.call-start = ((), (), s32[]{:S(2)}) async-start(), calls=%async_computation.8 | async-start | bytes 4718592 | tf_op jit(solution)/shard_map/all_gather | solution.py:131
  143.8 43.7 %copy-start.8 = (bf16[1,256,1024]{2,1,0:T(8,128)(2,1)S(1)}, bf16[1,256,1024]{2,1,0:T(8,128)(2,1)}, u32[]{:S(2)}) copy-start(bf16[1,256,1024]{2,1,0:T(8,128)(2,1)} %param.21) | copy-start | bytes 1572868
  143.8 98.5 %copy-start.6 = (bf16[1,256,1024]{2,1,0:T(8,128)(2,1)S(1)}, bf16[1,256,1024]{2,1,0:T(8,128)(2,1)}, u32[]{:S(2)}) copy-start(bf16[1,256,1024]{2,1,0:T(8,128)(2,1)} %param.25) | copy-start | bytes 1572868
  148.4 302.0 %reduce-scatter.8.cloned.1.call-start = ((), (), s32[]{:S(2)}) async-start(), calls=%async_computation.6 | async-start | bytes 2359296 | tf_op jit(solution)/shard_map/reduce_scatter | solution.py:109
  290.7 202.2 %reduce-scatter.10.cloned.1.call-start = ((), (), s32[]{:S(2)}) async-start(), calls=%async_computation.13 | async-start | bytes 4718592
  366.6 9.8 %copy-start.4 = (bf16[256,1024]{0,1:T(8,128)(2,1)S(1)}, bf16[256,1024]{0,1:T(8,128)(2,1)}, u32[]{:S(2)}) copy-start(bf16[256,1024]{0,1:T(8,128)(2,1)} %copy.51) | copy-start | bytes 1572868
  422.7 7.1 copy-start.5
  438.8 8.8 copy-start.7
  438.8 160.6 %all-reduce.5.cloned.1.call-start = ((), (), s32[]{:S(2)}) async-start(), calls=%async_computation.11 | async-start | bytes 8388608 | tf_op jit(solution)/shard_map/psum | solution.py:161
  450.4 299.0 %all-reduce.9.cloned.1.call-start = ((), (), s32[]{:S(2)}) async-start(), calls=%async_computation.14 | async-start | bytes 1572864 | tf_op jit(solution)/shard_map/psum | solution.py:18
  495.0 463.3 %all-reduce.7.cloned.1.call-start = ((), (), s32[]{:S(2)}) async-start(), calls=%async_computation.12 | async-start | bytes 8388608 | tf_op jit(solution)/shard_map/psum | solution.py:162
  599.4 11.9 %copy-start.3 = (bf16[1024,1024]{1,0:T(8,128)(2,1)S(1)}, bf16[1024,1024]{1,0:T(8,128)(2,1)}, u32[]{:S(2)}) copy-start(bf16[1024,1024]{1,0:T(8,128)(2,1)} %all-gather.17.cloned.1.call-done) | copy-start | bytes 6291460
  599.4 11.9 %copy-start.9 = (bf16[1,256,1024]{2,1,0:T(8,128)(2,1)S(1)}, bf16[1,256,1024]{2,1,0:T(8,128)(2,1)}, u32[]{:S(2)}) copy-start(bf16[1,256,1024]{2,1,0:T(8,128)(2,1)} %param.21) | copy-start | bytes 1572868
  609.4 10.5 %collective-permute-start = (bf16[128,1024]{1,0:T(8,128)(2,1)S(1)}, bf16[128,1024]{1,0:T(8,128)(2,1)S(1)}, u32[]{:S(2)}, u32[]{:S(2)}) collective-permute-start(bf16[128,1024]{1,0:T(8,128)(2,1)S(1)} %get-tuple-element.8), channel_id=1, source_target_pairs={{0,16},{16,32},{32,48},{48,64},{64,80},{80,96},{96,112},{112,128},... | collective-permute-start | bytes 786440 | tf_op jit(solution)/shard_map/ppermute | solution.py:13
  (3 other events, 15.2 us)
Sparse Core Ops, SparseCore 0:
  12.4 43.7 all-gather.6
  70.3 41.3 reduce-scatter.5
  290.8 69.1 reduce-scatter.7
  438.9 53.8 reduce-scatter.9
Sparse Core Ops, SparseCore 1:
  73.4 59.3 all-gather.10
  135.3 52.1 all-gather.14
  190.1 52.1 all-gather.16
  244.7 40.1 all-gather.8
  286.7 70.4 all-gather.12
  450.4 148.9 all-reduce.4
  602.5 146.7 all-reduce.8
  751.9 206.3 all-reduce.6
